TPU v7x, 512 devices: a whole 4x4x16 slice. The times are simulated.
512 devices in a mesh: wide: 64 (over z, x), narrow: 8 (over y, core).
Axes of the slice: x: 4, y: 4, z: 16, core: 2. Of those that a mesh axis runs over, the one named last changes fastest.
Arguments:
- hidden: bfloat16 [2048, 8192], P('wide', 'narrow'), may hold values from -6 to 6
- norm_gain: float32 [8192], P('narrow'), may hold values from 0.1 to 1.9
- head_weight: bfloat16 [8192, 32000], P('narrow', 'wide'), may hold values from -0.24 to 0.24
- diff_rows: bfloat16 [64, 8, 8, 32000], P('wide', 'narrow'), may hold values from -6 to 480
- slot_request: int32 [64, 8, 8], replicated, may hold values from 0 to 2047, as said below
- slot_code: int32 [64, 8, 8], replicated, may hold values from 1 to 8
- slot_count: int32 [64, 8], replicated, may hold values from 1 to 8, as said below
Outputs:
- log_probs: float32 [2048, 32000], P('narrow', 'wide')
Inputs may be any that keep to these rules, and one draw needn't show every extreme that they name: `slot_request`: within one pair, every request is named at most once. `slot_count`: slots at or beyond the count hold no row to use; in every draw some device uses all 8 slots.
All inputs are finite; a program needn't handle non-finite values.
Results may differ from a plain program's by a relative error of at most 0.0003.
Values may be sent and summed in bfloat16 or wider, within the bound.
A program may use at most 64 MiB of HBM per device.

v0:
```python
import jax
import jax.numpy as jnp
from jax import lax
from jax.sharding import PartitionSpec as P

D = 8192
epsilon = 1e-05


def combined_all(part, axis, combine):
    gathered = jax.tree.map(lambda a: lax.all_gather(a, axis), part)

    def take(source):
        return jax.tree.map(lambda a: lax.dynamic_index_in_dim(a, source, 0, False), gathered)

    return lax.fori_loop(
        1, lax.axis_size(axis), lambda source, state: combine(state, take(source)), take(0)
    )


def merge_pair(earlier, later):
    row_peak = jnp.maximum(earlier[0], later[0])
    summed = earlier[1] * jnp.exp(earlier[0] - row_peak) + later[1] * jnp.exp(later[0] - row_peak)
    return (row_peak, summed)


def body(hidden, norm_gain, head_weight, diff_rows, slot_request, slot_code, slot_count):
    values = hidden.astype(jnp.float32)
    squares = lax.psum(jnp.sum(values * values, axis=1), "narrow")
    scales = lax.rsqrt(squares / D + epsilon)
    normed = (values * scales[:, None] * norm_gain[None, :]).astype(jnp.bfloat16)
    partial_value = jnp.dot(
        lax.all_gather(normed, "wide", axis=0, tiled=True),
        head_weight,
        preferred_element_type=jnp.float32,
    )
    row_block = diff_rows[0, 0]
    arrived = lax.all_to_all(row_block, "wide", split_axis=1, concat_axis=0, tiled=True)
    slot_total = row_block.shape[0]
    active = jnp.arange(slot_total, dtype=jnp.int32)[None, None, :] < slot_count[:, :, None]
    weights = jnp.where(active, slot_code, 0).astype(jnp.float32) * 0.25
    base_block = lax.psum_scatter(partial_value, "narrow", scatter_dimension=0, tiled=True)
    owner_slices = lax.all_gather(arrived, "narrow", axis=0, tiled=True)
    targets = jnp.transpose(slot_request, (1, 0, 2)).reshape(-1)
    factor_all = jnp.transpose(weights, (1, 0, 2)).reshape(-1)
    block_rows = base_block.shape[0]
    offsets = targets - lax.axis_index("narrow") * block_rows
    owned = (offsets >= 0) & (offsets < block_rows)
    factors = jnp.where(owned, factor_all, 0.0)
    target_rows = jnp.where(owned, offsets, 0)
    own_block = base_block.at[target_rows].add(owner_slices.astype(jnp.float32) * factors[:, None])
    local_peak = jnp.max(own_block, axis=1)
    local_mass = jnp.sum(jnp.exp(own_block - local_peak[:, None]), axis=1)
    row_peak, row_mass = combined_all((local_peak, local_mass), "wide", merge_pair)
    log_total = row_peak + jnp.log(row_mass)
    return own_block - log_total[:, None]


def solution(mesh):
    placed = (
        P("wide", "narrow"),
        P("narrow"),
        P("narrow", "wide"),
        P("wide", "narrow", None, None),
        P(),
        P(),
        P(),
    )
    return jax.shard_map(
        body, mesh=mesh, in_specs=placed, out_specs=P("narrow", "wide"), check_vma=False
    )
```

profile of v0, /device:TPU:32, one launch (start us, length us, event | category | flops | bytes accessed | tf_op | source)
XLA Modules:
  0.0 463.4 jit_solution(9681761703783635985)
XLA Ops:
  6.5 0.0 copy-start
  6.5 1.0 fusion.4
  7.6 14.9 %psum.7 = f32[32]{0:T(128)S(1)} all-reduce(f32[32]{0:T(128)S(1)} %fusion.4), channel_id=1, replica_groups=mesh['wide'=64,'narrow'=8] {'narrow'}, use_global_device_ids=true, to_apply=%region_1.0 | all-reduce | flops 32 | bytes 256 | tf_op jit(solution)/shard_map/psum | solution.py:29
  22.5 1.6 fusion.6
  24.0 0.0 all-gather.7.cloned.1.call-update
  24.0 0.0 reduce-scatter.2.cloned.1.call-start
  24.1 147.9 %all-gather.7.cloned.1.call-done = bf16[2048,1024]{1,0:T(8,128)(2,1)} async-done(((bf16[32,1024]{1,0:T(8,128)(2,1)}), bf16[2048,1024]{1,0:T(8,128)(2,1)}) %all-gather.7.cloned.1.call-update) | async-done | bytes 4194320 | tf_op jit(solution)/shard_map/all_gather | solution.py:33
  172.0 6.5 %fusion.7 = f32[2048,500]{0,1:T(8,128)} fusion(bf16[2048,1024]{1,0:T(8,128)(2,1)} %all-gather.7.cloned.1.call-done, bf16[1024,500]{0,1:T(8,128)(2,1)S(1)} %copy-done), kind=kOutput, calls=%fused_computation.24 | convolution fusion | flops 2097152000 | bytes 9314304 | tf_op jit(solution)/shard_map/dot_general | solution.py:32
  178.5 0.0 reduce-scatter.2.cloned.1.call-update
  178.5 0.0 all-gather.9.cloned.1.call-start
  178.6 1.0 copy-done.1
  179.5 1.1 all_to_all.14
  180.7 0.3 copy.20
  181.0 32.8 %all_to_all.19 = bf16[8,64,500]{2,0,1:T(8,128)(2,1)} all-to-all(bf16[8,64,500]{2,0,1:T(8,128)(2,1)S(1)} %copy.20), channel_id=1, replica_groups=mesh['wide'=64,'narrow'=8] {'wide'}, dimensions={1} | all-to-all | bytes 1024000 | tf_op jit(solution)/shard_map/all_to_all | solution.py:38
  213.8 0.0 all-gather.9.cloned.1.call-update
  213.8 0.1 copy.19
  214.0 0.2 sub.63
  214.1 0.0 copy-done.3
  214.2 0.0 copy-done.4
  214.2 0.1 copy.21
  214.3 0.2 select_n.54
  214.5 5.4 %reduce-scatter.2.cloned.1.call-done = f32[256,500]{0,1:T(8,128)} async-done(((f32[2048,500]{0,1:T(8,128)}), f32[256,500]{0,1:T(8,128)}) %reduce-scatter.2.cloned.1.call-update) | async-done | bytes 512016 | tf_op jit(solution)/shard_map/reduce_scatter | solution.py:42
  219.9 1.2 copy.22
  221.1 39.4 %all-gather.9.cloned.1.call-done = bf16[4096,500]{1,0:T(8,128)(2,1)} async-done(((bf16[512,500]{1,0:T(8,128)(2,1)}), bf16[4096,500]{1,0:T(8,128)(2,1)}) %all-gather.9.cloned.1.call-update) | async-done | bytes 4096016 | tf_op jit(solution)/shard_map/all_gather | solution.py:43
  260.5 28.5 %scatter_custom_fusion = f32[256,500]{1,0:T(8,128)S(1)} fusion(f32[256,500]{1,0:T(8,128)S(1)} %copy.22, s32[4096]{0:T(1024)S(1)} %bitcast.35, bf16[4096,500]{1,0:T(8,128)(2,1)} %all-gather.9.cloned.1.call-done, f32[4096]{0:T(1024)S(1)} %select_n.54), kind=kCustom, calls=%fused_computation.4 | custom fusion | flops 6144000 | bytes 4624384 | tf_op jit(solution)/shard_map/scatter-add | solution.py:51
  288.9 0.2 copy.23
  289.1 0.1 reduce_max.9
  289.3 0.2 exponential_reduce_fusion
  289.5 82.5 %all-gather.2 = f32[64,1,256]{2,1,0:T(1,128)S(1)} all-gather(f32[1,1,256]{2,1,0:T(1,128)S(1)} %bitcast.36), channel_id=2, replica_groups=mesh['wide'=64,'narrow'=8] {'wide'}, dimensions={0}, use_global_device_ids=true | all-gather | bytes 66560 | tf_op jit(solution)/shard_map/all_gather | solution.py:11
  372.0 80.4 %all-gather.3 = f32[64,1,256]{2,1,0:T(1,128)S(1)} all-gather(f32[1,1,256]{2,1,0:T(1,128)S(1)} %bitcast.37), channel_id=3, replica_groups=mesh['wide'=64,'narrow'=8] {'wide'}, dimensions={0}, use_global_device_ids=true | all-gather | bytes 66560 | tf_op jit(solution)/shard_map/all_gather | solution.py:11
  452.4 3.6 while.17
  456.1 0.8 broadcast_subtract_fusion
  (142 shorter events, 2.1 us)
Async XLA Ops:
  6.5 165.5 %copy-start = (bf16[1024,500]{0,1:T(8,128)(2,1)S(1)}, bf16[1024,500]{0,1:T(8,128)(2,1)}, u32[]{:S(2)}) copy-start(bf16[1024,500]{0,1:T(8,128)(2,1)} %param.11) | copy-start | bytes 3072004
  6.5 165.5 %all-gather.7.cloned.1.call-start = ((), (), s32[]{:S(2)}) async-start(), calls=%async_computation.2 | async-start | bytes 4259840 | tf_op jit(solution)/shard_map/all_gather | solution.py:33
  24.0 195.8 %reduce-scatter.2.cloned.1.call-start = ((), (), s32[]{:S(2)}) async-start(), calls=%async_computation.3 | async-start | bytes 4644864 | tf_op jit(solution)/shard_map/reduce_scatter | solution.py:42
  178.5 1.0 copy-start.1
  178.5 35.3 %copy-start.2 = (s32[64,8,8]{0,2,1:T(8,128)S(1)}, s32[64,8,8]{0,2,1:T(8,128)}, u32[]{:S(2)}) copy-start(s32[64,8,8]{0,2,1:T(8,128)} %param.13) | copy-start | bytes 49156
  178.5 35.7 %copy-start.3 = (s32[64,8,8]{0,2,1:T(8,128)S(1)}, s32[64,8,8]{0,2,1:T(8,128)}, u32[]{:S(2)}) copy-start(s32[64,8,8]{0,2,1:T(8,128)} %param.14) | copy-start | bytes 49156
  178.5 35.7 %copy-start.4 = (s32[64,8]{0,1:T(8,128)S(1)}, s32[64,8]{0,1:T(8,128)}, u32[]{:S(2)}) copy-start(s32[64,8]{0,1:T(8,128)} %param.15) | copy-start | bytes 6148
  178.5 82.0 %all-gather.9.cloned.1.call-start = ((), (), s32[]{:S(2)}) async-start(), calls=%async_computation.4 | async-start | bytes 4718592 | tf_op jit(solution)/shard_map/all_gather | solution.py:43
Sparse Core Ops, SparseCore 0:
  24.2 147.8 all-gather.6
  178.6 41.1 reduce-scatter.1
  222.3 38.1 all-gather.8
where the time goes:
time: 464 us; the launch traced here: 463 us
  blocking collectives  211 us (45%)
  waiting for transfers between devices  193 us (42%)
  other arithmetic  33.6 us (7%)
  between operations  13.3 us (3%)
  matrix products  6.47 us (1%)
  local copies, waits for them, and re-layouts  5.1 us (1%)
    all_gather x2, blocking collectives, combined_all(): gathered = jax.tree.map(lambda a: lax.all_gather(a, axis), part)  163 us
    all_gather x1, waiting for transfers between devices, body(): lax.all_gather(normed, 'wide', axis=0, tiled=True)  148 us
    all_gather x1, waiting for transfers between devices, body(): owner_slices = lax.all_gather(arrived, 'narrow', axis=0, tiled=True)  39.4 us
    all_to_all x1, blocking collectives, body(): lax.all_to_all(row_block, 'wide', split_axis=1, concat_axis=0, tiled=True)  32.8 us
    scatter-add x1, other arithmetic, body(): base_block.at[target_rows]  28.5 us
    psum x1, blocking collectives, body(): squares = lax.psum(jnp.sum(values * values, axis=1), 'narrow')  14.9 us
  transfers between devices with their start and end apart: 3, of which 3 were waited for; matrix products, arithmetic and copies ran while one was open for 0% of the time, Pallas kernels for 0%

commit v1 on v0

--- a/solution.py
+++ b/solution.py
@@ -40,7 +40,14 @@
     active = jnp.arange(slot_total, dtype=jnp.int32)[None, None, :] < slot_count[:, :, None]
     weights = jnp.where(active, slot_code, 0).astype(jnp.float32) * 0.25
     base_block = lax.psum_scatter(partial_value, "narrow", scatter_dimension=0, tiled=True)
-    owner_slices = lax.all_gather(arrived, "narrow", axis=0, tiled=True)
+    ring = [arrived]
+    for hop in range(7):
+        ring.append(lax.ppermute(ring[-1], "narrow", [(dev, (dev + 1) % 8) for dev in range(8)]))
+    owner_slices = jnp.roll(
+        jnp.concatenate(ring[::-1], axis=0),
+        (lax.axis_index("narrow") + 1) * ring[0].shape[0],
+        axis=0,
+    )
     targets = jnp.transpose(slot_request, (1, 0, 2)).reshape(-1)
     factor_all = jnp.transpose(weights, (1, 0, 2)).reshape(-1)
     block_rows = base_block.shape[0]

time: 464 us -> 488 us (1.052)
  the two profiles are of different devices: /device:TPU:32 before, /device:TPU:2 now
where the time goes in v1:
time: 488 us; the launch traced here: 487 us
  waiting for transfers between devices  213 us (44%)
  blocking collectives  175 us (36%)
  other arithmetic  33.6 us (7%)
  local copies, waits for them, and re-layouts  25.3 us (5%)
  starting transfers between devices  18.7 us (4%)
  between operations  13.6 us (3%)
  matrix products  6.45 us (1%)
    all_gather x2, blocking collectives, combined_all(): gathered = jax.tree.map(lambda a: lax.all_gather(a, axis), part)  161 us
    all_gather x1, waiting for transfers between devices, body(): lax.all_gather(normed, 'wide', axis=0, tiled=True)  132 us
    ppermute x7, waiting for transfers between devices, body(): lax.ppermute(ring[-1], 'narrow', [(dev, (dev + 1) % 8) for dev in range(8)])  80.3 us
    scatter-add x1, other arithmetic, body(): base_block.at[target_rows]  28.5 us
    all_to_all x1, starting transfers between devices, body(): lax.all_to_all(row_block, 'wide', split_axis=1, concat_axis=0, tiled=True)  18.6 us
    unnamed x29, local copies, waits for them, and re-layouts  18.6 us
    psum x1, blocking collectives, body(): squares = lax.psum(jnp.sum(values * values, axis=1), 'narrow')  14.9 us
  transfers between devices with their start and end apart: 10, of which 8 were waited for; matrix products, arithmetic and copies ran while one was open for 5% of the time, Pallas kernels for 0%

profile of v1, /device:TPU:2, one launch (start us, length us, event | category | flops | bytes accessed | tf_op | source)
XLA Modules:
  0.0 487.5 jit_solution(7488544224328467300)
XLA Ops:
  6.5 1.0 fusion.5
  7.6 14.9 %psum.7 = f32[32]{0:T(128)S(1)} all-reduce(f32[32]{0:T(128)S(1)} %fusion.5), channel_id=1, replica_groups=mesh['wide'=64,'narrow'=8] {'narrow'}, use_global_device_ids=true, to_apply=%region_1.0 | all-reduce | flops 32 | bytes 256 | tf_op jit(solution)/shard_map/psum | solution.py:29
  22.5 1.6 fusion.7
  24.0 2.1 all_to_all.14
  26.1 1.1 copy.20
  27.2 18.6 %all-to-all-start = ((bf16[8,64,500]{2,0,1:T(8,128)(2,1)}), bf16[8,64,500]{2,0,1:T(8,128)(2,1)S(1)}, u32[]{:S(2)}, u32[]{:S(2)}) async-start(bf16[8,64,500]{2,0,1:T(8,128)(2,1)} %copy.20), calls=%async_computation.1 | async-start | bytes 1048576 | tf_op jit(solution)/shard_map/all_to_all | solution.py:38
  46.0 132.4 %all-gather.6.cloned.1.call-done = bf16[2048,1024]{1,0:T(8,128)(2,1)} async-done(((bf16[32,1024]{1,0:T(8,128)(2,1)}), bf16[2048,1024]{1,0:T(8,128)(2,1)}) %all-gather.6.cloned.1.call-update) | async-done | bytes 4194320 | tf_op jit(solution)/shard_map/all_gather | solution.py:33
  178.4 6.4 %fusion.8 = f32[2048,500]{0,1:T(8,128)} fusion(bf16[2048,1024]{1,0:T(8,128)(2,1)} %all-gather.6.cloned.1.call-done, bf16[1024,500]{0,1:T(8,128)(2,1)S(1)} %copy-done), kind=kOutput, calls=%fused_computation.41 | convolution fusion | flops 2097152000 | bytes 9314304 | tf_op jit(solution)/shard_map/dot_general | solution.py:32
  184.9 9.8 %collective-permute-done = bf16[512,500]{1,0:T(8,128)(2,1)S(1)} collective-permute-done((bf16[512,500]{1,0:T(8,128)(2,1)S(1)}, bf16[512,500]{1,0:T(8,128)(2,1)S(1)}, u32[]{:S(2)}, u32[]{:S(2)}) %collective-permute-start) | collective-permute-done | bytes 512032 | tf_op jit(solution)/shard_map/ppermute | solution.py:45
  194.7 13.9 %collective-permute-done.1 = bf16[512,500]{1,0:T(8,128)(2,1)S(1)} collective-permute-done((bf16[512,500]{1,0:T(8,128)(2,1)S(1)}, bf16[512,500]{1,0:T(8,128)(2,1)S(1)}, u32[]{:S(2)}, u32[]{:S(2)}) %collective-permute-start.1) | collective-permute-done | bytes 512032 | tf_op jit(solution)/shard_map/ppermute | solution.py:45
  208.6 15.1 %collective-permute-done.2 = bf16[512,500]{1,0:T(8,128)(2,1)S(1)} collective-permute-done((bf16[512,500]{1,0:T(8,128)(2,1)S(1)}, bf16[512,500]{1,0:T(8,128)(2,1)S(1)}, u32[]{:S(2)}, u32[]{:S(2)}) %collective-permute-start.2) | collective-permute-done | bytes 512032 | tf_op jit(solution)/shard_map/ppermute | solution.py:45
  223.8 12.0 %collective-permute-done.3 = bf16[512,500]{1,0:T(8,128)(2,1)S(1)} collective-permute-done((bf16[512,500]{1,0:T(8,128)(2,1)S(1)}, bf16[512,500]{1,0:T(8,128)(2,1)S(1)}, u32[]{:S(2)}, u32[]{:S(2)}) %collective-permute-start.3) | collective-permute-done | bytes 512032 | tf_op jit(solution)/shard_map/ppermute | solution.py:45
  236.6 9.9 %collective-permute-done.4 = bf16[512,500]{1,0:T(8,128)(2,1)} collective-permute-done((bf16[512,500]{1,0:T(8,128)(2,1)S(1)}, bf16[512,500]{1,0:T(8,128)(2,1)}, u32[]{:S(2)}, u32[]{:S(2)}) %collective-permute-start.4) | collective-permute-done | bytes 512032 | tf_op jit(solution)/shard_map/ppermute | solution.py:45
  247.2 9.5 %collective-permute-done.5 = bf16[512,500]{1,0:T(8,128)(2,1)} collective-permute-done((bf16[512,500]{1,0:T(8,128)(2,1)}, bf16[512,500]{1,0:T(8,128)(2,1)}, u32[]{:S(2)}, u32[]{:S(2)}) %collective-permute-start.5) | collective-permute-done | bytes 512032 | tf_op jit(solution)/shard_map/ppermute | solution.py:45
  256.7 10.0 %collective-permute-done.6 = bf16[512,500]{1,0:T(8,128)(2,1)S(1)} collective-permute-done((bf16[512,500]{1,0:T(8,128)(2,1)}, bf16[512,500]{1,0:T(8,128)(2,1)S(1)}, u32[]{:S(2)}, u32[]{:S(2)}) %collective-permute-start.6) | collective-permute-done | bytes 512032 | tf_op jit(solution)/shard_map/ppermute | solution.py:45
  267.5 1.9 constant_dynamic-update-slice_fusion.14
  269.4 1.9 constant_dynamic-update-slice_fusion.13
  271.3 1.9 constant_dynamic-update-slice_fusion.12
  273.2 0.8 constant_dynamic-update-slice_fusion.11
  274.0 0.8 constant_dynamic-update-slice_fusion.10
  275.7 0.8 constant_dynamic-update-slice_fusion.8
  276.5 0.8 constant_dynamic-update-slice_fusion.7
  277.3 1.9 constant_dynamic-update-slice_fusion.6
  279.2 1.9 constant_dynamic-update-slice_fusion.5
  281.9 0.9 constant_dynamic-update-slice_fusion.3
  282.8 0.8 constant_dynamic-update-slice_fusion.2
  284.4 0.9 constant_dynamic-update-slice_fusion
  285.3 1.2 copy.22
  286.5 28.5 %scatter_custom_fusion = f32[256,500]{1,0:T(8,128)S(1)} fusion(f32[256,500]{1,0:T(8,128)S(1)} %copy.22, s32[4096]{0:T(1024)S(1)} %bitcast.37, f32[4096]{0:T(1024)S(1)} %select_n.69, bf16[8192,500]{1,0:T(8,128)(2,1)} %constant_dynamic-update-slice_fusion, s32[]{:T(128)S(6)} %select_n.66, s32[]{:T(128)} %constant.82.clone.1), kind=kCustom, calls=%fused_computation.4 | custom fusion | flops 6144000 | bytes 4723204 | tf_op jit(solution)/shard_map/scatter-add | solution.py:58
  315.4 80.2 %all-gather.3 = f32[64,1,256]{2,1,0:T(1,128)S(1)} all-gather(f32[1,1,256]{2,1,0:T(1,128)S(1)} %bitcast.39), channel_id=3, replica_groups=mesh['wide'=64,'narrow'=8] {'wide'}, dimensions={0}, use_global_device_ids=true | all-gather | bytes 66560 | tf_op jit(solution)/shard_map/all_gather | solution.py:11
  395.6 80.3 %all-gather.2 = f32[64,1,256]{2,1,0:T(1,128)S(1)} all-gather(f32[1,1,256]{2,1,0:T(1,128)S(1)} %bitcast.38), channel_id=2, replica_groups=mesh['wide'=64,'narrow'=8] {'wide'}, dimensions={0}, use_global_device_ids=true | all-gather | bytes 66560 | tf_op jit(solution)/shard_map/all_gather | solution.py:11
  476.1 3.6 while.17
  (172 shorter events, 8.3 us)
Async XLA Ops:
  6.5 171.9 %copy-start = (bf16[1024,500]{0,1:T(8,128)(2,1)S(1)}, bf16[1024,500]{0,1:T(8,128)(2,1)}, u32[]{:S(2)}) copy-start(bf16[1024,500]{0,1:T(8,128)(2,1)} %param.11) | copy-start | bytes 3072004
  6.5 171.9 %all-gather.6.cloned.1.call-start = ((), (), s32[]{:S(2)}) async-start(), calls=%async_computation.2 | async-start | bytes 4259840 | tf_op jit(solution)/shard_map/all_gather | solution.py:33
  27.2 157.6 %all-to-all-start = ((bf16[8,64,500]{2,0,1:T(8,128)(2,1)}), bf16[8,64,500]{2,0,1:T(8,128)(2,1)S(1)}, u32[]{:S(2)}, u32[]{:S(2)}) async-start(bf16[8,64,500]{2,0,1:T(8,128)(2,1)} %copy.20), calls=%async_computation.1 | async-start | bytes 1048576 | tf_op jit(solution)/shard_map/all_to_all | solution.py:38
  45.9 200.7 %copy-start.3 = (s32[64,8,8]{0,2,1:T(8,128)S(1)}, s32[64,8,8]{0,2,1:T(8,128)}, u32[]{:S(2)}) copy-start(s32[64,8,8]{0,2,1:T(8,128)} %param.13) | copy-start | bytes 49156
  45.9 201.0 %copy-start.4 = (s32[64,8,8]{0,2,1:T(8,128)S(1)}, s32[64,8,8]{0,2,1:T(8,128)}, u32[]{:S(2)}) copy-start(s32[64,8,8]{0,2,1:T(8,128)} %param.14) | copy-start | bytes 49156
  45.9 201.0 %copy-start.5 = (s32[64,8]{0,1:T(8,128)S(1)}, s32[64,8]{0,1:T(8,128)}, u32[]{:S(2)}) copy-start(s32[64,8]{0,1:T(8,128)} %param.15) | copy-start | bytes 6148
  45.9 239.4 %reduce-scatter.2.cloned.1.call-start = ((), (), s32[]{:S(2)}) async-start(), calls=%async_computation.3 | async-start | bytes 4644864 | tf_op jit(solution)/shard_map/reduce_scatter | solution.py:42
  184.9 9.8 %collective-permute-start = (bf16[512,500]{1,0:T(8,128)(2,1)S(1)}, bf16[512,500]{1,0:T(8,128)(2,1)S(1)}, u32[]{:S(2)}, u32[]{:S(2)}) collective-permute-start(bf16[512,500]{1,0:T(8,128)(2,1)S(1)} %bitcast.30), channel_id=1, source_target_pairs={{0,1},{1,2},{2,3},{3,4},{4,5},{5,6},{6,7},{7,0},{8,9},{9,10},{10,1... | collective-permute-start | bytes 1536008 | tf_op jit(solution)/shard_map/ppermute | solution.py:45
  194.7 13.9 %collective-permute-start.1 = (bf16[512,500]{1,0:T(8,128)(2,1)S(1)}, bf16[512,500]{1,0:T(8,128)(2,1)S(1)}, u32[]{:S(2)}, u32[]{:S(2)}) collective-permute-start(bf16[512,500]{1,0:T(8,128)(2,1)S(1)} %collective-permute-done), channel_id=1, source_target_pairs={{0,1},{1,2},{2,3},{3,4},{4,5},{5,6},{6,7},{7,0},{8,9},{9,10},{10,1... | collective-permute-start | bytes 1536008 | tf_op jit(solution)/shard_map/ppermute | solution.py:45
  208.6 15.1 %collective-permute-start.2 = (bf16[512,500]{1,0:T(8,128)(2,1)S(1)}, bf16[512,500]{1,0:T(8,128)(2,1)S(1)}, u32[]{:S(2)}, u32[]{:S(2)}) collective-permute-start(bf16[512,500]{1,0:T(8,128)(2,1)S(1)} %collective-permute-done.1), channel_id=1, source_target_pairs={{0,1},{1,2},{2,3},{3,4},{4,5},{5,6},{6,7},{7,0},{8,9},{9,10},{10,1... | collective-permute-start | bytes 1536008 | tf_op jit(solution)/shard_map/ppermute | solution.py:45
  223.8 12.0 %collective-permute-start.3 = (bf16[512,500]{1,0:T(8,128)(2,1)S(1)}, bf16[512,500]{1,0:T(8,128)(2,1)S(1)}, u32[]{:S(2)}, u32[]{:S(2)}) collective-permute-start(bf16[512,500]{1,0:T(8,128)(2,1)S(1)} %collective-permute-done.2), channel_id=1, source_target_pairs={{0,1},{1,2},{2,3},{3,4},{4,5},{5,6},{6,7},{7,0},{8,9},{9,10},{10,1... | collective-permute-start | bytes 1536008 | tf_op jit(solution)/shard_map/ppermute | solution.py:45
  235.8 0.8 copy-start.1
  236.6 9.9 %collective-permute-start.4 = (bf16[512,500]{1,0:T(8,128)(2,1)S(1)}, bf16[512,500]{1,0:T(8,128)(2,1)}, u32[]{:S(2)}, u32[]{:S(2)}) collective-permute-start(bf16[512,500]{1,0:T(8,128)(2,1)S(1)} %collective-permute-done.3), channel_id=1, source_target_pairs={{0,1},{1,2},{2,3},{3,4},{4,5},{5,6},{6,7},{7,0},{8,9},{9,10},{10,1... | collective-permute-start | bytes 1536008 | tf_op jit(solution)/shard_map/ppermute | solution.py:45
  246.5 10.1 %collective-permute-start.5 = (bf16[512,500]{1,0:T(8,128)(2,1)}, bf16[512,500]{1,0:T(8,128)(2,1)}, u32[]{:S(2)}, u32[]{:S(2)}) collective-permute-start(bf16[512,500]{1,0:T(8,128)(2,1)} %collective-permute-done.4), channel_id=1, source_target_pairs={{0,1},{1,2},{2,3},{3,4},{4,5},{5,6},{6,7},{7,0},{8,9},{9,10},{10,1... | collective-permute-start | bytes 1536008 | tf_op jit(solution)/shard_map/ppermute | solution.py:45
  247.2 33.9 %copy-start.2 = (bf16[512,500]{1,0:T(8,128)(2,1)S(1)}, bf16[512,500]{1,0:T(8,128)(2,1)}, u32[]{:S(2)}) copy-start(bf16[512,500]{1,0:T(8,128)(2,1)} %copy-done.1) | copy-start | bytes 1536004
  256.7 10.0 %collective-permute-start.6 = (bf16[512,500]{1,0:T(8,128)(2,1)}, bf16[512,500]{1,0:T(8,128)(2,1)S(1)}, u32[]{:S(2)}, u32[]{:S(2)}) collective-permute-start(bf16[512,500]{1,0:T(8,128)(2,1)} %collective-permute-done.5), channel_id=1, source_target_pairs={{0,1},{1,2},{2,3},{3,4},{4,5},{5,6},{6,7},{7,0},{8,9},{9,10},{10,1... | collective-permute-start | bytes 1536008 | tf_op jit(solution)/shard_map/ppermute | solution.py:45
Sparse Core Ops, SparseCore 0:
  24.2 154.1 all-gather.5
  185.0 49.0 reduce-scatter.1
